TPU v7x, 256 devices: a whole 4x4x8 slice. The times are simulated.
256 devices in a mesh: dp: 8 (over z_lo, x), ctx: 32 (over z_hi, y, core).
Axes of the slice: x: 4, y: 4, z: 8 (z_hi: 4, z_lo: 2; z = z_hi * 2 + z_lo), core: 2. Of those that a mesh axis runs over, the one named last changes fastest.
Arguments:
- tokens: bfloat16 [8, 4096, 4096], P('dp', 'ctx'), may hold values from -6 to 6
- proj_weight: bfloat16 [4096, 512], P('dp'), may hold values from -0.09375 to 0.09375
- values: bfloat16 [8, 4096, 2048], P('dp', 'ctx'), may hold values from -60 to 60
- grad_out: bfloat16 [8, 4096, 2048], P('dp', 'ctx'), may hold values from -6 to 6
Outputs:
- attended: bfloat16 [8, 4096, 2048], P('dp', 'ctx')
- grad_tokens: bfloat16 [8, 4096, 4096], P('dp', 'ctx')
- grad_values: bfloat16 [8, 4096, 2048], P('dp', 'ctx')
- grad_proj: float32 [4096, 512], P(('dp', 'ctx'))
All inputs are finite; a program needn't handle non-finite values.
Results may differ from a plain program's by a relative error of at most 0.0049.
Values may be sent and summed in bfloat16 or wider, within the bound.
A program may use at most 192 MiB of HBM per device.

v0:
```python
import jax
import jax.numpy as jnp
from jax import lax
from jax.sharding import PartitionSpec as P

H = 16
F = 16
DH = 128
HIGHEST = lax.Precision.HIGHEST
QUAD_SCALE = 0.17677669529663687
EPSILON = 1e-05


def features(inputs):
    count_heads, count_rows, count_feat = inputs.shape
    linear = jnp.swapaxes(inputs, 1, 2) * 0.5
    square = (inputs[:, :, :, None] * inputs[:, :, None, :]).reshape(
        count_heads, count_rows, count_feat * count_feat
    )
    square = jnp.swapaxes(square, 1, 2) * QUAD_SCALE
    constant_row = jnp.ones((count_heads, 1, count_rows), inputs.dtype)
    return jnp.concatenate([constant_row, linear, square], axis=1)


def block_kernel(query_part, key_part):
    count_rows = query_part.shape[1]
    causal = lax.broadcasted_iota(jnp.int32, (count_rows, count_rows), 0) >= lax.broadcasted_iota(
        jnp.int32, (count_rows, count_rows), 1
    )
    scores = jnp.einsum("htf,hsf->hts", query_part, key_part, precision=HIGHEST) * 0.25
    kernel = jnp.where(causal, 1.0 + scores + 0.5 * scores * scores, 0.0)
    return (causal, scores, kernel)


def normalize(numerator):
    inv_rms = lax.rsqrt(jnp.mean(numerator * numerator, axis=-1, keepdims=True) + EPSILON)
    return (inv_rms, numerator * inv_rms)


def grad_normalize(inv_rms, normed, upstream):
    return inv_rms * (upstream - normed * jnp.mean(normed * upstream, axis=-1, keepdims=True))


def local_backward(
    query_part,
    key_part,
    value_part,
    grad_num,
    causal,
    scores,
    kernel,
    pull_query,
    pull_key,
    feat_key,
    prefix,
    suffix,
):
    mixing = jnp.where(
        causal, jnp.einsum("htd,hsd->hts", grad_num, value_part, precision=HIGHEST), 0.0
    )
    slope = mixing * (1.0 + scores)
    grad_query = jnp.einsum("hts,hsf->htf", slope, key_part, precision=HIGHEST) * 0.25
    grad_key = jnp.einsum("hts,htf->hsf", slope, query_part, precision=HIGHEST) * 0.25
    grad_query = (
        grad_query + pull_query(jnp.einsum("hed,htd->het", prefix, grad_num, precision=HIGHEST))[0]
    )
    grad_key = (
        grad_key + pull_key(jnp.einsum("hed,htd->het", suffix, value_part, precision=HIGHEST))[0]
    )
    grad_value = jnp.einsum("hts,htd->hsd", kernel, grad_num, precision=HIGHEST)
    grad_value = grad_value + jnp.einsum("het,hed->htd", feat_key, suffix, precision=HIGHEST)
    return (grad_query, grad_key, grad_value)


def split_heads(matrix, size):
    return jnp.swapaxes(matrix.reshape(matrix.shape[0], -1, size), 0, 1)


def merge_heads(blocked):
    return jnp.swapaxes(blocked, 0, 1).reshape(blocked.shape[1], -1)


def local(tokens, proj_weight, values, grad_out):
    token_rows = tokens[0]
    query_cols = H * F
    projected = jnp.dot(
        token_rows,
        lax.all_gather(proj_weight, "dp", axis=0, tiled=True),
        preferred_element_type=jnp.float32,
    )
    query_part = split_heads(projected[:, :query_cols], F)
    key_part = split_heads(projected[:, query_cols:], F)
    value_part = split_heads(values[0].astype(jnp.float32), DH)
    upstream = split_heads(grad_out[0].astype(jnp.float32), DH)
    feat_query, pull_query = jax.vjp(features, query_part)
    feat_key, pull_key = jax.vjp(features, key_part)
    local_term = jnp.einsum("het,htd->hed", feat_key, value_part, precision=HIGHEST)
    columns_in = lax.all_to_all(
        local_term.reshape(1, -1), "ctx", split_axis=1, concat_axis=0, tiled=True
    )
    shifted = jnp.concatenate([jnp.zeros_like(columns_in[:1]), columns_in[:-1]], axis=0)
    running = jnp.cumsum(shifted, axis=0)
    prefix = lax.all_to_all(running, "ctx", split_axis=0, concat_axis=1, tiled=True).reshape(
        local_term.shape
    )
    causal, scores, kernel = block_kernel(query_part, key_part)
    numerator = jnp.einsum("hts,hsd->htd", kernel, value_part, precision=HIGHEST)
    numerator = numerator + jnp.einsum("het,hed->htd", feat_query, prefix, precision=HIGHEST)
    inv_rms, normed = normalize(numerator)
    attended = merge_heads(normed).astype(jnp.bfloat16)
    grad_num = grad_normalize(inv_rms, normed, upstream)
    carried = jnp.einsum("het,htd->hed", feat_query, grad_num, precision=HIGHEST)
    later_in = lax.all_to_all(
        carried.reshape(1, -1), "ctx", split_axis=1, concat_axis=0, tiled=True
    )
    later_shift = jnp.concatenate([later_in[1:], jnp.zeros_like(later_in[:1])], axis=0)
    later_running = jnp.cumsum(later_shift[::-1], axis=0)[::-1]
    suffix = lax.all_to_all(later_running, "ctx", split_axis=0, concat_axis=1, tiled=True).reshape(
        carried.shape
    )
    grad_query, grad_key, grad_value = local_backward(
        query_part,
        key_part,
        value_part,
        grad_num,
        causal,
        scores,
        kernel,
        pull_query,
        pull_key,
        feat_key,
        prefix,
        suffix,
    )
    grad_proj_rows = jnp.concatenate(
        [merge_heads(grad_query), merge_heads(grad_key)], axis=1
    ).astype(jnp.bfloat16)
    grad_tokens = lax.dot_general(
        grad_proj_rows,
        lax.all_gather(proj_weight, "dp", axis=0, tiled=True),
        (((1,), (1,)), ((), ())),
        preferred_element_type=jnp.float32,
    ).astype(jnp.bfloat16)
    grad_proj = lax.psum_scatter(
        lax.dot_general(
            token_rows, grad_proj_rows, (((0,), (0,)), ((), ())), preferred_element_type=jnp.float32
        ),
        ("dp", "ctx"),
        scatter_dimension=0,
        tiled=True,
    )
    grad_values = merge_heads(grad_value).astype(jnp.bfloat16)
    return (attended[None], grad_tokens[None], grad_values[None], grad_proj)


def solution(mesh):
    return jax.shard_map(
        local,
        mesh=mesh,
        in_specs=(P("dp", "ctx", None), P("dp", None), P("dp", "ctx", None), P("dp", "ctx", None)),
        out_specs=(
            P("dp", "ctx", None),
            P("dp", "ctx", None),
            P("dp", "ctx", None),
            P(("dp", "ctx"), None),
        ),
        check_vma=False,
    )
```

profile of v0, /device:TPU:32, one launch (start us, length us, event | category | flops | bytes accessed | tf_op | source)
XLA Modules:
  0.0 2036.4 jit_solution(6238759362847132041)
XLA Ops:
  9.1 57.5 %all-gather.2.cloned.1.call-done = bf16[4096,512]{1,0:T(8,128)(2,1)} async-done(((bf16[512,512]{1,0:T(8,128)(2,1)}), bf16[4096,512]{1,0:T(8,128)(2,1)}) %all-gather.2.cloned.1.call-update) | async-done | bytes 4194320 | tf_op jit(solution)/shard_map/all_gather | solution.py:88
  66.6 2.9 fusion.20
  71.9 3.5 fusion.3
  75.4 4.0 all_to_all.45
  79.4 65.7 %all_to_all.51 = f32[1,32,17472]{2,0,1:T(1,128)S(1)} all-to-all(f32[1,32,17472]{2,0,1:T(1,128)S(1)} %all_to_all.45), channel_id=1, replica_groups=mesh['dp'=8,'ctx'=32] {'ctx'}, dimensions={1} | all-to-all | bytes 4472832 | tf_op jit(solution)/shard_map/all_to_all | solution.py:98
  145.1 2.6 fusion.1
  147.6 4.2 all-to-all-start.1
  151.9 2.2 copy.39
  157.4 3.7 fusion.60
  161.0 2.6 multiply_multiply_fusion.1
  163.6 43.2 %all-to-all-done.1 = f32[32,1,17472]{2,1,0:T(1,128)S(1)} async-done(((f32[32,1,17472]{2,1,0:T(1,128)}), f32[32,1,17472]{2,1,0:T(1,128)S(1)}, u32[]{:S(2)}, u32[]{:S(2)}) %all-to-all-start.1) | async-done | bytes 2236448 | tf_op jit(solution)/shard_map/all_to_all | solution.py:103
  206.8 7.3 reduce
  214.1 2.4 reshape.141
  216.6 7.7 fusion.5
  227.7 5.2 fusion.4
  233.0 5.1 all_to_all.46
  238.1 60.0 %all_to_all.52 = f32[1,32,17472]{2,0,1:T(1,128)S(1)} all-to-all(f32[1,32,17472]{2,0,1:T(1,128)} %all_to_all.46), channel_id=1, replica_groups=mesh['dp'=8,'ctx'=32] {'ctx'}, dimensions={1} | all-to-all | bytes 4472832 | tf_op jit(solution)/shard_map/all_to_all | solution.py:113
  299.9 60.9 %rev.6 = f32[32,17472]{1,0:T(8,128)} reverse(f32[32,17472]{1,0:T(8,128)} %concatenate.16), dimensions={0} | reverse | bytes 4472832 | tf_op jit(solution)/shard_map/rev | solution.py:117
  360.8 4.9 reduce_window_sum.21
  365.7 60.9 %rev.7 = f32[32,17472]{1,0:T(8,128)} reverse(f32[32,17472]{1,0:T(8,128)} %reduce_window_sum.21), dimensions={0} | reverse | bytes 4472832 | tf_op jit(solution)/shard_map/rev | solution.py:117
  426.6 5.3 copy.44
  431.9 4.8 all-to-all-start.3
  437.0 5.5 fusion.61
  448.5 42.8 %all-to-all-done.3 = f32[32,1,17472]{2,1,0:T(1,128)} async-done(((f32[32,1,17472]{2,1,0:T(1,128)}), f32[32,1,17472]{2,1,0:T(1,128)}, u32[]{:S(2)}, u32[]{:S(2)}) %all-to-all-start.3) | async-done | bytes 2236448 | tf_op jit(solution)/shard_map/all_to_all | solution.py:118
  491.3 8.6 reduce.1
  499.8 3.2 reshape.144
  503.0 3.8 fusion.25
  509.3 4.5 convolution_bitcast_fusion
  513.8 9.2 copy.54
  527.3 7.6 fusion.2
  539.0 4.7 fusion
  543.7 1485.6 %reduce-scatter.4.cloned.1.call-done = f32[16,512]{1,0:T(8,128)} async-done(((f32[4096,512]{1,0:T(8,128)}), f32[16,512]{1,0:T(8,128)}) %reduce-scatter.4.cloned.1.call-update) | async-done | bytes 32784
  (66 shorter events, 29.8 us)
Async XLA Ops:
  7.2 59.4 %copy-start = (bf16[1,128,4096]{2,1,0:T(8,128)(2,1)S(1)}, bf16[1,128,4096]{2,1,0:T(8,128)(2,1)}, u32[]{:S(2)}) copy-start(bf16[1,128,4096]{2,1,0:T(8,128)(2,1)} %param.4) | copy-start | bytes 3145732
  7.2 59.4 %all-gather.2.cloned.1.call-start = ((), (), s32[]{:S(2)}) async-start(), calls=%async_computation.5 | async-start | bytes 4718592 | tf_op jit(solution)/shard_map/all_gather | solution.py:88
  9.1 61.5 %copy-start.7 = (bf16[16,8,16,128]{3,2,1,0:T(8,128)(2,1)}, bf16[16,8,16,128]{3,2,1,0:T(8,128)(2,1)S(1)}, u32[]{:S(2)}) copy-start(bf16[16,8,16,128]{3,2,1,0:T(8,128)(2,1)S(1)} %copy.57) | copy-start | bytes 1572868
  70.2 0.6 copy-start.14
  70.5 1.3 copy-start.3
  147.6 59.2 %all-to-all-start.1 = ((f32[32,1,17472]{2,1,0:T(1,128)}), f32[32,1,17472]{2,1,0:T(1,128)S(1)}, u32[]{:S(2)}, u32[]{:S(2)}) async-start(f32[32,1,17472]{2,1,0:T(1,128)} %fusion.1), calls=%async_computation.1 | async-start | bytes 4489216 | tf_op jit(solution)/shard_map/all_to_all | solution.py:103
  216.6 7.8 copy-start.1
  216.6 7.8 copy-start.4
  216.6 7.8 copy-start.8
  224.3 1.4 copy-start.10
  225.7 1.1 copy-start.6
  225.8 2.0 copy-start.2
  225.8 1.9 copy-start.16
  431.9 59.3 %all-to-all-start.3 = ((f32[32,1,17472]{2,1,0:T(1,128)}), f32[32,1,17472]{2,1,0:T(1,128)}, u32[]{:S(2)}, u32[]{:S(2)}) async-start(f32[32,1,17472]{2,1,0:T(1,128)} %copy.44), calls=%async_computation.3 | async-start | bytes 4489216 | tf_op jit(solution)/shard_map/all_to_all | solution.py:118
  436.7 1592.6 %reduce-scatter.4.cloned.1.call-start = ((), (), s32[]{:S(2)}) async-start(), calls=%async_computation.6 | async-start | bytes 8421376
  442.5 0.9 copy-start.13
  443.4 1.2 copy-start.5
  443.4 1.4 copy-start.9
  445.8 1.0 copy-start.11
  507.1 1.2 copy-start.12
  523.0 4.2 copy-start.15
Sparse Core Ops, SparseCore 0:
  9.8 56.6 all-gather.1
  523.1 1506.1 reduce-scatter.3
where the time goes:
time: 2050 us; the launch traced here: 2040 us
  waiting for transfers between devices  1630 us (80%)
  local copies, waits for them, and re-layouts  168 us (8%)
  blocking collectives  126 us (6%)
  matrix products  56.2 us (3%)
  other arithmetic  33 us (2%)
    unnamed x3, waiting for transfers between devices  1490 us
    rev x2, local copies, waits for them, and re-layouts, local(): later_running = jnp.cumsum(later_shift[::-1], axis=0)[::-1]  122 us
    all_to_all x1, blocking collectives, local(): lax.all_to_all(local_term.reshape(1, -1), 'ctx', split_axis=1, concat_axi...  65.7 us
    all_to_all x1, blocking collectives, local(): lax.all_to_all(carried.reshape(1, -1), 'ctx', split_axis=1, concat_axis=0...  60 us
    all_gather x1, waiting for transfers between devices, local(): lax.all_gather(proj_weight, 'dp', axis=0, tiled=True)  57.5 us
    all_to_all x1, waiting for transfers between devices, local(): lax.all_to_all(running, 'ctx', split_axis=0, concat_axis=1, tiled=True)  43.2 us
    all_to_all x1, waiting for transfers between devices, local(): lax.all_to_all(later_running, 'ctx', split_axis=0, concat_axis=1, tiled=T...  42.8 us
  transfers between devices with their start and end apart: 4, of which 4 were waited for; matrix products, arithmetic and copies ran while one was open for 2% of the time, Pallas kernels for 0%

commit v1 on v0

--- a/solution.py
+++ b/solution.py
@@ -9,6 +9,12 @@
 HIGHEST = lax.Precision.HIGHEST
 QUAD_SCALE = 0.17677669529663687
 EPSILON = 1e-05
+
+
+def finish_the_targets(point):
+    return jnp.concatenate(
+        lax.all_to_all(jnp.stack([point] * lax.axis_size("dp"), axis=0), "dp", 0, 0), axis=0
+    )
 
 
 def features(inputs):
@@ -84,9 +90,7 @@
     token_rows = tokens[0]
     query_cols = H * F
     projected = jnp.dot(
-        token_rows,
-        lax.all_gather(proj_weight, "dp", axis=0, tiled=True),
-        preferred_element_type=jnp.float32,
+        token_rows, finish_the_targets(proj_weight), preferred_element_type=jnp.float32
     )
     query_part = split_heads(projected[:, :query_cols], F)
     key_part = split_heads(projected[:, query_cols:], F)

time: 2050 us -> 2080 us (1.015)
  waiting for transfers between devices: 1630 us -> 1690 us
  blocking collectives: 126 us -> 66.3 us
    all_to_all x0 -> x2, waiting for transfers between devices: none -> 120 us  [the longest x1 72.4 us: local(): lax.all_to_all(carried.reshape(1, -1), 'ctx', split_axis=1, concat_axis=0...]
    all_to_all x1 -> x0, blocking collectives: 60 us -> none  [local(): lax.all_to_all(carried.reshape(1, -1), 'ctx', split_axis=1, concat_axis=0...]
    all_gather x1, waiting for transfers between devices: 57.5 us -> 0.01 us  [local(): lax.all_gather(proj_weight, 'dp', axis=0, tiled=True)]
  transfers between devices with their start and end apart: 4 -> 6, of which waited for: 4 -> 5; matrix products, arithmetic and copies ran while one was open for 2% -> 10% of each run, Pallas kernels for 0% -> 0%
where the time goes in v1:
time: 2080 us; the launch traced here: 2060 us
  waiting for transfers between devices  1690 us (81%)
  local copies, waits for them, and re-layouts  172 us (8%)
  blocking collectives  66.3 us (3%)
  matrix products  56.2 us (3%)
  other arithmetic  33 us (2%)
  starting transfers between devices  22.8 us (1%)
    unnamed x3, waiting for transfers between devices  1490 us
    rev x2, local copies, waits for them, and re-layouts, local(): later_running = jnp.cumsum(later_shift[::-1], axis=0)[::-1]  122 us
    all_to_all x1, waiting for transfers between devices, local(): lax.all_to_all(carried.reshape(1, -1), 'ctx', split_axis=1, concat_axis=0...  72.4 us
    all_to_all x1, blocking collectives, local(): lax.all_to_all(local_term.reshape(1, -1), 'ctx', split_axis=1, concat_axi...  66.3 us
    all_to_all x1, waiting for transfers between devices, finish_the_targets(): lax.all_to_all(jnp.stack([point] * lax.axis_size('dp'), axis=0), 'dp', 0, 0)  47.4 us
    all_to_all x1, waiting for transfers between devices, local(): lax.all_to_all(running, 'ctx', split_axis=0, concat_axis=1, tiled=True)  43.3 us
  transfers between devices with their start and end apart: 6, of which 5 were waited for; matrix products, arithmetic and copies ran while one was open for 10% of the time, Pallas kernels for 0%

profile of v1, /device:TPU:32, one launch (start us, length us, event | category | flops | bytes accessed | tf_op | source)
XLA Modules:
  0.0 2057.5 jit_solution(18259418175108732489)
XLA Ops:
  8.0 3.5 stack.2
  11.5 6.4 all-to-all-start
  18.0 47.4 %all-to-all-done = bf16[8,512,512]{2,1,0:T(8,128)(2,1)} async-done(((bf16[8,512,512]{2,1,0:T(8,128)(2,1)}), bf16[8,512,512]{2,1,0:T(8,128)(2,1)}, u32[]{:S(2)}, u32[]{:S(2)}) %all-to-all-start) | async-done | bytes 4194336 | tf_op jit(solution)/shard_map/all_to_all | solution.py:16
  65.4 2.9 fusion.20
  70.8 3.5 fusion.3
  74.2 4.0 all_to_all.49
  78.2 66.3 %all_to_all.56 = f32[1,32,17472]{2,0,1:T(1,128)S(1)} all-to-all(f32[1,32,17472]{2,0,1:T(1,128)S(1)} %all_to_all.49), channel_id=1, replica_groups=mesh['dp'=8,'ctx'=32] {'ctx'}, dimensions={1} | all-to-all | bytes 4472832 | tf_op jit(solution)/shard_map/all_to_all | solution.py:102
  144.6 2.6 fusion.1
  147.2 4.2 all-to-all-start.2
  156.9 3.7 fusion.60
  163.2 43.3 %all-to-all-done.2 = f32[32,1,17472]{2,1,0:T(1,128)S(1)} async-done(((f32[32,1,17472]{2,1,0:T(1,128)}), f32[32,1,17472]{2,1,0:T(1,128)S(1)}, u32[]{:S(2)}, u32[]{:S(2)}) %all-to-all-start.2) | async-done | bytes 2236448 | tf_op jit(solution)/shard_map/all_to_all | solution.py:107
  206.5 7.3 reduce
  216.2 7.7 fusion.5
  227.4 5.2 fusion.4
  232.6 5.1 all_to_all.50
  237.7 4.8 all-to-all-start.3
  243.3 72.4 %all-to-all-done.3 = f32[1,32,17472]{2,0,1:T(1,128)} async-done(((f32[1,32,17472]{2,0,1:T(1,128)}), f32[1,32,17472]{2,0,1:T(1,128)}, u32[]{:S(2)}, u32[]{:S(2)}) %all-to-all-start.3) | async-done | bytes 2236448 | tf_op jit(solution)/shard_map/all_to_all | solution.py:117
  319.2 61.0 %rev.6 = f32[32,17472]{1,0:T(8,128)} reverse(f32[32,17472]{1,0:T(8,128)} %concatenate.16), dimensions={0} | reverse | bytes 4472832 | tf_op jit(solution)/shard_map/rev | solution.py:121
  380.2 4.9 reduce_window_sum.21
  385.1 61.0 %rev.7 = f32[32,17472]{1,0:T(8,128)} reverse(f32[32,17472]{1,0:T(8,128)} %reduce_window_sum.21), dimensions={0} | reverse | bytes 4472832 | tf_op jit(solution)/shard_map/rev | solution.py:121
  446.0 5.4 copy.44
  451.4 7.1 all-to-all-start.4
  458.7 5.5 fusion.61
  470.3 38.0 %all-to-all-done.4 = f32[32,1,17472]{2,1,0:T(1,128)} async-done(((f32[32,1,17472]{2,1,0:T(1,128)}), f32[32,1,17472]{2,1,0:T(1,128)}, u32[]{:S(2)}, u32[]{:S(2)}) %all-to-all-start.4) | async-done | bytes 2236448 | tf_op jit(solution)/shard_map/all_to_all | solution.py:122
  508.2 8.6 reduce.1
  516.8 3.2 reshape.150
  520.0 3.8 fusion.25
  526.3 4.5 convolution_bitcast_fusion
  530.7 9.2 copy.54
  544.3 7.6 fusion.2
  556.0 4.7 fusion
  560.6 1489.2 %reduce-scatter.4.cloned.1.call-done = f32[16,512]{1,0:T(8,128)} async-done(((f32[4096,512]{1,0:T(8,128)}), f32[16,512]{1,0:T(8,128)}) %reduce-scatter.4.cloned.1.call-update) | async-done | bytes 32784
  (72 shorter events, 37.6 us)
Async XLA Ops:
  8.0 57.4 %copy-start = (bf16[1,128,4096]{2,1,0:T(8,128)(2,1)S(1)}, bf16[1,128,4096]{2,1,0:T(8,128)(2,1)}, u32[]{:S(2)}) copy-start(bf16[1,128,4096]{2,1,0:T(8,128)(2,1)} %param.4) | copy-start | bytes 3145732
  11.5 6.4 copy-start.17
  11.5 53.9 %all-to-all-start = ((bf16[8,512,512]{2,1,0:T(8,128)(2,1)}), bf16[8,512,512]{2,1,0:T(8,128)(2,1)}, u32[]{:S(2)}, u32[]{:S(2)}) async-start(bf16[8,512,512]{2,1,0:T(8,128)(2,1)} %stack.2), calls=%async_computation | async-start | bytes 8388608 | tf_op jit(solution)/shard_map/all_to_all | solution.py:16
  18.0 51.4 %copy-start.7 = (bf16[16,8,16,128]{3,2,1,0:T(8,128)(2,1)}, bf16[16,8,16,128]{3,2,1,0:T(8,128)(2,1)S(1)}, u32[]{:S(2)}) copy-start(bf16[16,8,16,128]{3,2,1,0:T(8,128)(2,1)S(1)} %copy.57) | copy-start | bytes 1572868
  69.1 0.7 copy-start.14
  69.4 1.4 copy-start.3
  147.2 59.3 %all-to-all-start.2 = ((f32[32,1,17472]{2,1,0:T(1,128)}), f32[32,1,17472]{2,1,0:T(1,128)S(1)}, u32[]{:S(2)}, u32[]{:S(2)}) async-start(f32[32,1,17472]{2,1,0:T(1,128)} %fusion.1), calls=%async_computation.2 | async-start | bytes 4489216 | tf_op jit(solution)/shard_map/all_to_all | solution.py:107
  216.2 7.8 copy-start.1
  216.2 7.8 copy-start.4
  216.2 7.8 copy-start.8
  224.0 1.4 copy-start.10
  225.4 1.1 copy-start.6
  225.4 2.0 copy-start.2
  225.4 1.9 copy-start.16
  237.7 78.0 %all-to-all-start.3 = ((f32[1,32,17472]{2,0,1:T(1,128)}), f32[1,32,17472]{2,0,1:T(1,128)}, u32[]{:S(2)}, u32[]{:S(2)}) async-start(f32[1,32,17472]{2,0,1:T(1,128)} %all_to_all.50), calls=%async_computation.3 | async-start | bytes 4489216 | tf_op jit(solution)/shard_map/all_to_all | solution.py:117
  242.5 313.4 %all-gather.2.cloned.1.call-start = ((), (), s32[]{:S(2)}) async-start(), calls=%async_computation.6 | async-start | bytes 4718592 | tf_op jit(solution)/shard_map/all_gather | solution.py:144
  451.4 56.8 %all-to-all-start.4 = ((f32[32,1,17472]{2,1,0:T(1,128)}), f32[32,1,17472]{2,1,0:T(1,128)}, u32[]{:S(2)}, u32[]{:S(2)}) async-start(f32[32,1,17472]{2,1,0:T(1,128)} %copy.44), calls=%async_computation.4 | async-start | bytes 4489216 | tf_op jit(solution)/shard_map/all_to_all | solution.py:122
  458.5 1591.3 %reduce-scatter.4.cloned.1.call-start = ((), (), s32[]{:S(2)}) async-start(), calls=%async_computation.7 | async-start | bytes 8421376
  464.3 0.9 copy-start.13
  465.2 1.2 copy-start.5
  465.2 1.4 copy-start.9
  467.5 1.0 copy-start.11
  524.1 1.2 copy-start.12
  540.0 4.2 copy-start.15
Sparse Core Ops, SparseCore 0:
  245.2 89.9 all-gather.1
Sparse Core Ops, SparseCore 1:
  540.1 1509.6 reduce-scatter.3
